TPU v7x, 32 devices: a whole 2x2x4 slice. The times are simulated.
32 devices in a mesh: regroup: 2 (over y), loop: 4 (over z), replica: 4 (over x, core).
Axes of the slice: x: 2, y: 2, z: 4, core: 2. Of those that a mesh axis runs over, the one named last changes fastest.
Arguments:
- features: bfloat16 [4, 4, 1024, 256], P('replica', 'loop', None, 'regroup'), may hold values from -6 to 6
- weight: bfloat16 [256, 256], replicated, may hold values from -0.375 to 0.375
- tiles: bfloat16 [4, 4, 2, 32, 128, 128], P('replica', 'loop', 'regroup'), may hold values from 0 to 1, as said below
- tile_row: int32 [4, 4, 2, 32], P('replica', 'loop', 'regroup'), may hold values from 0 to 3, as said below
- tile_col: int32 [4, 4, 2, 32], P('replica', 'loop', 'regroup'), may hold values from 0 to 3, as said below
- tile_width: int32 [4, 4, 2, 32], P('replica', 'loop', 'regroup'), may hold values from 0 to 128, as said below
- cotangent: bfloat16 [4, 4, 2, 512, 256], P('replica', 'loop', 'regroup'), may hold values from -6 to 6
Outputs:
- output: bfloat16 [4, 4, 2, 512, 256], P('replica', 'loop', 'regroup')
- grad_feat: bfloat16 [4, 4, 1024, 256], P('replica', 'loop', None, 'regroup')
- grad_weight: float32 [256, 256], replicated
Inputs may be any that keep to these rules, and one draw needn't show every extreme that they name: `tiles`: entries are 0 or between 0.25 and 1. `tile_row`: slot k < 4 of every device names cell block k. tile_col[r, l, g, s] is l - 1, l or l + 1 modulo 4. `tile_width`: each device's live slots come first, from 4 to 32 of them; some device has exactly 4 live and some all 32; slot 0 is live with width 128.
All inputs are finite; a program needn't handle non-finite values.
Results may differ from a plain program's by a relative error of at most 0.013.
Values may be sent and summed in bfloat16 or wider, within the bound.
A program may use at most 64 MiB of HBM per device.

v0:
```python
import math
import jax
import jax.numpy as jnp
from jax import lax
from jax.sharding import PartitionSpec as P

EPSILON = 1e-06


def shifted(block, axis, distance):
    devices = range(lax.axis_size(axis))
    route = [((i - distance) % len(devices), i) for i in devices]
    return lax.ppermute(block, axis, route)


def rms_scale(values):
    return values * lax.rsqrt(jnp.mean(values * values, axis=-1, keepdims=True) + EPSILON)


def per_device(features, weight, tiles, tile_row, tile_col, tile_width, cotangent):
    cell_rows = lax.all_to_all(features, "regroup", split_axis=2, concat_axis=3, tiled=True)[0, 0]
    cells, width = cell_rows.shape
    edge = tiles.shape[-1]
    blocks = cells // edge
    loops = lax.axis_size("loop")
    high = lax.Precision.HIGHEST
    rows_idx = tile_row[0, 0, 0]
    cols_idx = tile_col[0, 0, 0]
    widths = tile_width[0, 0, 0]
    column = jnp.arange(edge, dtype=jnp.int32)
    live_tiles = jnp.where(
        column[None, None, :] < widths[:, None, None], tiles[0, 0, 0], jnp.zeros((), tiles.dtype)
    )
    row_hot = (rows_idx[:, None] == jnp.arange(blocks, dtype=jnp.int32)[None, :]).astype(
        jnp.float32
    )
    row_sums = jnp.sum(live_tiles, axis=2, dtype=jnp.float32)
    cell_deg = 1.0 + jnp.einsum("tr,ti->ri", row_hot, row_sums, precision=high).reshape(cells)
    cell_root = jnp.sqrt(cell_deg)[:, None]
    col_tile_sums = jnp.sum(live_tiles, axis=1, dtype=jnp.float32)

    def to_nets(values, hot):
        gathered = values.reshape(blocks, edge, width)[rows_idx]
        per_tile = jnp.einsum(
            "tij,tif->tjf", live_tiles, gathered, preferred_element_type=jnp.float32
        )
        return jnp.einsum("tc,tjf->cjf", hot, per_tile, precision=high)

    def from_nets(blocked, index):
        gathered = blocked[index]
        per_tile = jnp.einsum(
            "tij,tjf->tif", live_tiles, gathered, preferred_element_type=jnp.float32
        )
        return jnp.einsum("tr,tif->rif", row_hot, per_tile, precision=high).reshape(cells, width)

    mixed = jnp.dot(cell_rows, weight, preferred_element_type=jnp.float32).astype(jnp.bfloat16)
    scaled = (mixed.astype(jnp.float32) / cell_root).astype(jnp.bfloat16)
    place = (cols_idx - lax.axis_index("loop") + loops) % loops
    net_index = jnp.where(place == 0, 1, jnp.where(place == 1, 2, 0)).astype(jnp.int32)
    near_hot = (net_index[:, None] == jnp.arange(3, dtype=jnp.int32)[None, :]).astype(jnp.float32)
    near_terms = to_nets(scaled, near_hot).astype(jnp.bfloat16)
    near_degs = jnp.einsum("tc,tj->cj", near_hot, col_tile_sums, precision=high).astype(
        jnp.bfloat16
    )
    below = shifted((near_terms[2], near_degs[2]), "loop", 1)
    above = shifted((near_terms[0], near_degs[0]), "loop", -1)
    totals = (
        near_terms[1].astype(jnp.float32)
        + below[0].astype(jnp.float32)
        + above[0].astype(jnp.float32)
    )
    degrees = (
        near_degs[1].astype(jnp.float32)
        + below[1].astype(jnp.float32)
        + above[1].astype(jnp.float32)
    )
    net_deg = (1.0 + degrees)[:, None]
    own_feat = (totals / net_deg).astype(jnp.bfloat16)
    prev_feat = shifted(own_feat, "loop", 1)
    next_feat = shifted(own_feat, "loop", -1)
    net_feat = jnp.stack([prev_feat, own_feat, next_feat])
    gathered_z = from_nets(net_feat, net_index) / cell_root
    normed, norm_back = jax.vjp(rms_scale, gathered_z)
    before = mixed.astype(jnp.float32) + normed
    output = jax.nn.silu(before).astype(jnp.bfloat16)
    sigmoid_v = jax.nn.sigmoid(before)
    grad_before = (
        cotangent[0, 0, 0].astype(jnp.float32) * sigmoid_v * (1.0 + before * (1.0 - sigmoid_v))
    )
    grad_z = norm_back(grad_before)[0]
    grad_scaled = (grad_z / cell_root).astype(jnp.bfloat16)
    grad_near = to_nets(grad_scaled, near_hot).astype(jnp.bfloat16)
    grad_below = shifted(grad_near[2], "loop", 1)
    grad_above = shifted(grad_near[0], "loop", -1)
    grad_sum_own = (
        grad_near[1].astype(jnp.float32)
        + grad_below.astype(jnp.float32)
        + grad_above.astype(jnp.float32)
    )
    grad_own = (grad_sum_own / net_deg).astype(jnp.bfloat16)
    grad_prev = shifted(grad_own, "loop", 1)
    grad_next = shifted(grad_own, "loop", -1)
    grad_net = jnp.stack([grad_prev, grad_own, grad_next])
    grad_mixed = (grad_before + from_nets(grad_net, net_index) / cell_root).astype(jnp.bfloat16)
    grad_rows = jnp.einsum(
        "cg,fg->cf", grad_mixed, weight, preferred_element_type=jnp.float32
    ).astype(jnp.bfloat16)
    grad_feat = lax.all_to_all(
        grad_rows[None, None], "regroup", split_axis=3, concat_axis=2, tiled=True
    )
    weight_term = jnp.einsum("cf,cg->fg", cell_rows, grad_mixed, preferred_element_type=jnp.float32)
    weight_part = lax.psum_scatter(
        weight_term, ("regroup", "loop"), scatter_dimension=0, tiled=True
    )
    weight_part = lax.psum(weight_part, "replica")
    weight_sum = lax.all_gather(weight_part, ("regroup", "loop"), axis=0, tiled=True)
    total_cells = cells * lax.axis_size("regroup") * loops * lax.axis_size("replica")
    grad_weight = weight_sum * (1.0 / math.sqrt(total_cells))
    return (output[None, None, None], grad_feat, grad_weight)


def solution(mesh):
    return jax.shard_map(
        per_device,
        mesh=mesh,
        in_specs=(
            P("replica", "loop", None, "regroup"),
            P(),
            P("replica", "loop", "regroup", None, None, None),
            P("replica", "loop", "regroup", None),
            P("replica", "loop", "regroup", None),
            P("replica", "loop", "regroup", None),
            P("replica", "loop", "regroup", None, None),
        ),
        out_specs=(
            P("replica", "loop", "regroup", None, None),
            P("replica", "loop", None, "regroup"),
            P(),
        ),
        check_vma=False,
    )
```

profile of v0, /device:TPU:0, one launch (start us, length us, event | category | flops | bytes accessed | tf_op | source)
XLA Modules:
  0.0 198.6 jit_solution(6420533877653232573)
XLA Ops:
  8.6 1.6 convert_reduce_fusion
  11.0 3.0 %collective-permute-start.2 = (bf16[128]{0:T(256)(128)(2,1)}, bf16[128]{0:T(256)(128)(2,1)}, u32[]{:S(2)}, u32[]{:S(2)}) collective-permute-start(bf16[128]{0:T(256)(128)(2,1)} %get-tuple-element.22), channel_id=1, source_target_pairs={{12,0},{0,4},{4,8},{8,12},{13,1},{1,5},{5,9},{9,13},{14,2},{2,6},{... | collective-permute-start | bytes 776 | tf_op jit(solution)/shard_map/ppermute | solution.py:13
  14.0 2.0 %collective-permute-start.3 = (bf16[128]{0:T(256)(128)(2,1)}, bf16[128]{0:T(256)(128)(2,1)}, u32[]{:S(2)}, u32[]{:S(2)}) collective-permute-start(bf16[128]{0:T(256)(128)(2,1)} %get-tuple-element.23), channel_id=1, source_target_pairs={{4,0},{8,4},{12,8},{0,12},{5,1},{9,5},{13,9},{1,13},{6,2},{10,6},{... | collective-permute-start | bytes 776 | tf_op jit(solution)/shard_map/ppermute | solution.py:13
  16.0 1.4 copy.130
  17.9 2.3 %reduce.1 = bf16[1024,128]{1,0:T(8,128)(2,1)S(1)} reduce(bf16[1024,1,1,128]{3,2,1,0:T(2,128)(2,1)S(1)} %bitcast.136, bf16[]{:T(256)} %broadcast.232), dimensions={1,2}, to_apply=%bitcast.131.reduce_sub_computation | reduce | bytes 524290
  20.9 3.4 %all-to-all-start = ((bf16[2,2,32768]{2,1,0:T(2,128)(2,1)}), bf16[2,2,32768]{2,1,0:T(2,128)(2,1)S(1)}, u32[]{:S(2)}, u32[]{:S(2)}) async-start(bf16[2,2,32768]{2,1,0:T(2,128)(2,1)} %reshape.232), calls=%async_computation | async-start | bytes 524288 | tf_op jit(solution)/shard_map/all_to_all | solution.py:21
  25.9 3.6 %all-to-all-done = bf16[2,2,32768]{2,1,0:T(2,128)(2,1)S(1)} async-done(((bf16[2,2,32768]{2,1,0:T(2,128)(2,1)}), bf16[2,2,32768]{2,1,0:T(2,128)(2,1)S(1)}, u32[]{:S(2)}, u32[]{:S(2)}) %all-to-all-start) | async-done | bytes 262176 | tf_op jit(solution)/shard_map/all_to_all | solution.py:21
  30.0 1.1 divide_convert_fusion
  33.1 3.8 %fusion.9 = bf16[3,128,256]{2,0,1:T(4,128)(2,1)S(1)} fusion(f32[32,128,256]{2,1,0:T(8,128)S(1)} %fusion.23, s32[32]{0:T(128)S(1)} %copy-done.10), kind=kOutput, calls=%fused_computation.17 | convolution fusion | flops 37847136 | bytes 4391040 | tf_op jit(solution)/shard_map/tc,tjf->cjf/dot_general | solution.py:47
  37.3 2.1 %collective-permute-start.1 = (bf16[128,256]{1,0:T(8,128)(2,1)S(1)}, bf16[128,256]{1,0:T(8,128)(2,1)S(1)}, u32[]{:S(2)}, u32[]{:S(2)}) collective-permute-start(bf16[128,256]{1,0:T(8,128)(2,1)S(1)} %bitcast.146), channel_id=1, source_target_pairs={{4,0},{8,4},{12,8},{0,12},{5,1},{9,5},{13,9},{1,13},{6,2},{10,6},{... | collective-permute-start | bytes 196616 | tf_op jit(solution)/shard_map/ppermute | solution.py:13
  40.0 1.6 collective-permute-done.1
  41.6 3.8 %collective-permute-done = bf16[128,256]{1,0:T(8,128)(2,1)S(1)} collective-permute-done((bf16[128,256]{1,0:T(8,128)(2,1)S(1)}, bf16[128,256]{1,0:T(8,128)(2,1)S(1)}, u32[]{:S(2)}, u32[]{:S(2)}) %collective-permute-start) | collective-permute-done | bytes 65568 | tf_op jit(solution)/shard_map/ppermute | solution.py:13
  45.6 2.0 %collective-permute-start.4 = (bf16[128,256]{1,0:T(8,128)(2,1)S(1)}, bf16[128,256]{1,0:T(8,128)(2,1)S(1)}, u32[]{:S(2)}, u32[]{:S(2)}) collective-permute-start(bf16[128,256]{1,0:T(8,128)(2,1)S(1)} %fusion.27), channel_id=1, source_target_pairs={{12,0},{0,4},{4,8},{8,12},{13,1},{1,5},{5,9},{9,13},{14,2},{2,6},{... | collective-permute-start | bytes 196616 | tf_op jit(solution)/shard_map/ppermute | solution.py:13
  47.6 2.2 %collective-permute-done.5 = bf16[128,256]{1,0:T(8,128)(2,1)S(1)} collective-permute-done((bf16[128,256]{1,0:T(8,128)(2,1)S(1)}, bf16[128,256]{1,0:T(8,128)(2,1)S(1)}, u32[]{:S(2)}, u32[]{:S(2)}) %collective-permute-start.5) | collective-permute-done | bytes 65568 | tf_op jit(solution)/shard_map/ppermute | solution.py:13
  49.8 2.0 %collective-permute-done.4 = bf16[128,256]{1,0:T(8,128)(2,1)S(1)} collective-permute-done((bf16[128,256]{1,0:T(8,128)(2,1)S(1)}, bf16[128,256]{1,0:T(8,128)(2,1)S(1)}, u32[]{:S(2)}, u32[]{:S(2)}) %collective-permute-start.4) | collective-permute-done | bytes 65568 | tf_op jit(solution)/shard_map/ppermute | solution.py:13
  53.5 4.0 %fusion.19 = (f32[4,128]{0,1:T(8,128)S(1)}, f32[4,128,256]{2,0,1:T(4,128)S(1)}) fusion(f32[4,128]{0,1:T(8,128)S(1)} %copy-done.8, f32[32,128,256]{2,1,0:T(8,128)S(1)} %fusion.22, s32[32]{0:T(128)S(1)} %bitcast.156), kind=kOutput, calls=%fused_computation.39 | convolution fusion | flops 50724480 | bytes 4722816 | tf_op jit(solution)/shard_map/tr,tif->rif/dot_general | solution.py:54
  57.7 1.1 multiply_reduce_fusion
  61.1 3.8 %fusion.2 = bf16[3,128,256]{2,0,1:T(4,128)(2,1)S(1)} fusion(f32[32,128,256]{2,1,0:T(8,128)S(1)} %fusion.21, s32[32]{0:T(128)S(1)} %copy-done.11), kind=kOutput, calls=%fused_computation.6 | convolution fusion | flops 37748832 | bytes 4391040 | tf_op jit(solution)/shard_map/tc,tjf->cjf/dot_general | solution.py:47
  65.0 3.8 %collective-permute-start.7 = (bf16[128,256]{1,0:T(8,128)(2,1)S(1)}, bf16[128,256]{1,0:T(8,128)(2,1)S(1)}, u32[]{:S(2)}, u32[]{:S(2)}) collective-permute-start(bf16[128,256]{1,0:T(8,128)(2,1)S(1)} %get-tuple-element.21), channel_id=1, source_target_pairs={{4,0},{8,4},{12,8},{0,12},{5,1},{9,5},{13,9},{1,13},{6,2},{10,6},{... | collective-permute-start | bytes 196616 | tf_op jit(solution)/shard_map/ppermute | solution.py:13
  68.9 2.2 %collective-permute-done.6 = bf16[128,256]{1,0:T(8,128)(2,1)S(1)} collective-permute-done((bf16[128,256]{1,0:T(8,128)(2,1)S(1)}, bf16[128,256]{1,0:T(8,128)(2,1)S(1)}, u32[]{:S(2)}, u32[]{:S(2)}) %collective-permute-start.6) | collective-permute-done | bytes 65568 | tf_op jit(solution)/shard_map/ppermute | solution.py:13
  71.2 4.2 %collective-permute-start.9 = (bf16[128,256]{1,0:T(8,128)(2,1)S(1)}, bf16[128,256]{1,0:T(8,128)(2,1)S(1)}, u32[]{:S(2)}, u32[]{:S(2)}) collective-permute-start(bf16[128,256]{1,0:T(8,128)(2,1)S(1)} %fusion.30), channel_id=1, source_target_pairs={{4,0},{8,4},{12,8},{0,12},{5,1},{9,5},{13,9},{1,13},{6,2},{10,6},{... | collective-permute-start | bytes 196616 | tf_op jit(solution)/shard_map/ppermute | solution.py:13
  75.4 1.9 collective-permute-done.9
  77.3 4.2 %collective-permute-done.8 = bf16[128,256]{1,0:T(8,128)(2,1)S(1)} collective-permute-done((bf16[128,256]{1,0:T(8,128)(2,1)S(1)}, bf16[128,256]{1,0:T(8,128)(2,1)S(1)}, u32[]{:S(2)}, u32[]{:S(2)}) %collective-permute-start.8) | collective-permute-done | bytes 65568 | tf_op jit(solution)/shard_map/ppermute | solution.py:13
  82.9 3.8 %fusion = f32[4,128,256]{2,0,1:T(4,128)S(1)} fusion(f32[32,128,256]{2,1,0:T(8,128)S(1)} %fusion.20, s32[32]{0:T(128)S(1)} %bitcast.157), kind=kOutput, calls=%fused_computation.4 | convolution fusion | flops 50331776 | bytes 4718720 | tf_op jit(solution)/shard_map/tr,tif->rif/dot_general | solution.py:54
  87.9 0.8 copy.102
  89.5 2.2 %reduce.2 = bf16[256,512]{1,0:T(8,128)(2,1)S(1)} reduce(bf16[256,1,1,512]{3,2,1,0:T(2,128)(2,1)S(1)} %bitcast.137, bf16[]{:T(256)} %broadcast.232), dimensions={1,2}, to_apply=%bitcast.110.reduce_sub_computation | reduce | bytes 524290
  91.9 7.6 %all_to_all.33 = bf16[2,2,32768]{2,1,0:T(2,128)(2,1)S(1)} all-to-all(bf16[2,2,32768]{2,1,0:T(2,128)(2,1)S(1)} %reshape.234), channel_id=1, replica_groups=mesh['regroup'=2,'loop'=4,'replica'=4] {'regroup'}, dimensions={0} | all-to-all | bytes 524288 | tf_op jit(solution)/shard_map/all_to_all | solution.py:108
  99.8 0.8 copy.98
  100.6 46.8 %reduce-scatter.4.cloned.1.call-done = f32[32,256]{1,0:T(8,128)} async-done(((f32[256,256]{1,0:T(8,128)}), f32[32,256]{1,0:T(8,128)}) %reduce-scatter.4.cloned.1.call-update) | async-done | bytes 32784
  147.4 0.9 copy.103
  148.2 11.5 %psum.7 = f32[32,256]{0,1:T(8,128)S(1)} all-reduce(f32[32,256]{0,1:T(8,128)S(1)} %copy.103), channel_id=1, replica_groups=mesh['regroup'=2,'loop'=4,'replica'=4] {'replica'}, use_global_device_ids=true, to_apply=%region_5.6 | all-reduce | flops 8192 | bytes 65536 | tf_op jit(solution)/shard_map/psum | solution.py:115
  159.8 31.3 %all_gather.3 = f32[256,256]{1,0:T(8,128)S(1)} all-gather(f32[32,256]{1,0:T(8,128)S(1)} %copy.99), channel_id=1, replica_groups=mesh['regroup'=2,'loop'=4,'replica'=4] {'regroup','loop'}, dimensions={0}, use_global_device_ids=true | all-gather | bytes 294912 | tf_op jit(solution)/shard_map/all_gather | solution.py:116
  (96 shorter events, 17.3 us)
Async XLA Ops:
  7.2 22.9 %copy-start = (bf16[256,256]{1,0:T(8,128)(2,1)S(1)}, bf16[256,256]{1,0:T(8,128)(2,1)}, u32[]{:S(2)}) copy-start(bf16[256,256]{1,0:T(8,128)(2,1)} %param.8) | copy-start | bytes 393220
  7.2 17.3 %copy-start.18 = (s32[1,1,1,32]{3,2,1,0:T(1,128)S(1)}, s32[1,1,1,32]{3,2,1,0:T(1,128)}, u32[]{:S(2)}) copy-start(s32[1,1,1,32]{3,2,1,0:T(1,128)} %param.11) | copy-start | bytes 388
  7.2 17.8 %copy-start.14 = (s32[1,1,1,32]{3,2,1,0:T(1,128)S(1)}, s32[1,1,1,32]{3,2,1,0:T(1,128)}, u32[]{:S(2)}) copy-start(s32[1,1,1,32]{3,2,1,0:T(1,128)} %param.10) | copy-start | bytes 388
  8.6 16.4 %copy-start.9 = (s32[32]{0:T(128)}, s32[32]{0:T(128)S(1)}, u32[]{:S(2)}) copy-start(s32[32]{0:T(128)S(1)} %compare_select_fusion.8) | copy-start | bytes 388
  11.0 28.4 %collective-permute-start.2 = (bf16[128]{0:T(256)(128)(2,1)}, bf16[128]{0:T(256)(128)(2,1)}, u32[]{:S(2)}, u32[]{:S(2)}) collective-permute-start(bf16[128]{0:T(256)(128)(2,1)} %get-tuple-element.22), channel_id=1, source_target_pairs={{12,0},{0,4},{4,8},{8,12},{13,1},{1,5},{5,9},{9,13},{14,2},{2,6},{... | collective-permute-start | bytes 776 | tf_op jit(solution)/shard_map/ppermute | solution.py:13
  14.0 25.4 %collective-permute-start.3 = (bf16[128]{0:T(256)(128)(2,1)}, bf16[128]{0:T(256)(128)(2,1)}, u32[]{:S(2)}, u32[]{:S(2)}) collective-permute-start(bf16[128]{0:T(256)(128)(2,1)} %get-tuple-element.23), channel_id=1, source_target_pairs={{4,0},{8,4},{12,8},{0,12},{5,1},{9,5},{13,9},{1,13},{6,2},{10,6},{... | collective-permute-start | bytes 776 | tf_op jit(solution)/shard_map/ppermute | solution.py:13
  20.9 8.6 %all-to-all-start = ((bf16[2,2,32768]{2,1,0:T(2,128)(2,1)}), bf16[2,2,32768]{2,1,0:T(2,128)(2,1)S(1)}, u32[]{:S(2)}, u32[]{:S(2)}) async-start(bf16[2,2,32768]{2,1,0:T(2,128)(2,1)} %reshape.232), calls=%async_computation | async-start | bytes 524288 | tf_op jit(solution)/shard_map/all_to_all | solution.py:21
  24.4 123.0 %reduce-scatter.4.cloned.1.call-start = ((), (), s32[]{:S(2)}) async-start(), calls=%async_computation.3 | async-start | bytes 294912
  30.0 1.1 copy-start.4
  31.1 1.2 copy-start.1
  32.3 0.8 copy-start.10
  33.1 14.5 %copy-start.17 = (s32[32]{0:T(128)S(1)}, s32[32]{0:T(128)}, u32[]{:S(2)}) copy-start(s32[32]{0:T(128)} %fusion.43) | copy-start | bytes 388
  37.3 4.3 %collective-permute-start.1 = (bf16[128,256]{1,0:T(8,128)(2,1)S(1)}, bf16[128,256]{1,0:T(8,128)(2,1)S(1)}, u32[]{:S(2)}, u32[]{:S(2)}) collective-permute-start(bf16[128,256]{1,0:T(8,128)(2,1)S(1)} %bitcast.146), channel_id=1, source_target_pairs={{4,0},{8,4},{12,8},{0,12},{5,1},{9,5},{13,9},{1,13},{6,2},{10,6},{... | collective-permute-start | bytes 196616 | tf_op jit(solution)/shard_map/ppermute | solution.py:13
  39.4 6.1 %collective-permute-start = (bf16[128,256]{1,0:T(8,128)(2,1)S(1)}, bf16[128,256]{1,0:T(8,128)(2,1)S(1)}, u32[]{:S(2)}, u32[]{:S(2)}) collective-permute-start(bf16[128,256]{1,0:T(8,128)(2,1)S(1)} %bitcast.145), channel_id=1, source_target_pairs={{12,0},{0,4},{4,8},{8,12},{13,1},{1,5},{5,9},{9,13},{14,2},{2,6},{... | collective-permute-start | bytes 196616 | tf_op jit(solution)/shard_map/ppermute | solution.py:13
  40.0 11.9 %copy-start.12 = (f32[128]{0:T(128)}, f32[128]{0:T(128)S(1)}, u32[]{:S(2)}) copy-start(f32[128]{0:T(128)S(1)} %fusion.48) | copy-start | bytes 1540
  45.5 4.3 %collective-permute-start.5 = (bf16[128,256]{1,0:T(8,128)(2,1)S(1)}, bf16[128,256]{1,0:T(8,128)(2,1)S(1)}, u32[]{:S(2)}, u32[]{:S(2)}) collective-permute-start(bf16[128,256]{1,0:T(8,128)(2,1)S(1)} %fusion.27), channel_id=1, source_target_pairs={{4,0},{8,4},{12,8},{0,12},{5,1},{9,5},{13,9},{1,13},{6,2},{10,6},{... | collective-permute-start | bytes 196616 | tf_op jit(solution)/shard_map/ppermute | solution.py:13
  45.6 6.3 %collective-permute-start.4 = (bf16[128,256]{1,0:T(8,128)(2,1)S(1)}, bf16[128,256]{1,0:T(8,128)(2,1)S(1)}, u32[]{:S(2)}, u32[]{:S(2)}) collective-permute-start(bf16[128,256]{1,0:T(8,128)(2,1)S(1)} %fusion.27), channel_id=1, source_target_pairs={{12,0},{0,4},{4,8},{8,12},{13,1},{1,5},{5,9},{9,13},{14,2},{2,6},{... | collective-permute-start | bytes 196616 | tf_op jit(solution)/shard_map/ppermute | solution.py:13
  52.6 0.8 copy-start.8
  52.6 0.8 copy-start.15
  53.4 4.2 %copy-start.6 = (f32[512,256]{1,0:T(8,128)S(1)}, f32[512,256]{1,0:T(8,128)}, u32[]{:S(2)}) copy-start(f32[512,256]{1,0:T(8,128)} %get-tuple-element.25) | copy-start | bytes 1572868
  53.5 4.2 %copy-start.7 = (bf16[1,1,1,512,256]{4,3,2,1,0:T(8,128)(2,1)S(1)}, bf16[1,1,1,512,256]{4,3,2,1,0:T(8,128)(2,1)}, u32[]{:S(2)}) copy-start(bf16[1,1,1,512,256]{4,3,2,1,0:T(8,128)(2,1)} %param.13) | copy-start | bytes 786436
  58.8 0.8 copy-start.2
  60.3 0.8 copy-start.11
  61.1 10.0 %copy-start.13 = (f32[128]{0:T(128)S(1)}, f32[128]{0:T(128)}, u32[]{:S(2)}) copy-start(f32[128]{0:T(128)} %copy-done.12) | copy-start | bytes 1540
  65.0 6.1 %collective-permute-start.6 = (bf16[128,256]{1,0:T(8,128)(2,1)S(1)}, bf16[128,256]{1,0:T(8,128)(2,1)S(1)}, u32[]{:S(2)}, u32[]{:S(2)}) collective-permute-start(bf16[128,256]{1,0:T(8,128)(2,1)S(1)} %get-tuple-element.20), channel_id=1, source_target_pairs={{12,0},{0,4},{4,8},{8,12},{13,1},{1,5},{5,9},{9,13},{14,2},{2,6},{... | collective-permute-start | bytes 196616 | tf_op jit(solution)/shard_map/ppermute | solution.py:13
  65.0 6.1 %collective-permute-start.7 = (bf16[128,256]{1,0:T(8,128)(2,1)S(1)}, bf16[128,256]{1,0:T(8,128)(2,1)S(1)}, u32[]{:S(2)}, u32[]{:S(2)}) collective-permute-start(bf16[128,256]{1,0:T(8,128)(2,1)S(1)} %get-tuple-element.21), channel_id=1, source_target_pairs={{4,0},{8,4},{12,8},{0,12},{5,1},{9,5},{13,9},{1,13},{6,2},{10,6},{... | collective-permute-start | bytes 196616 | tf_op jit(solution)/shard_map/ppermute | solution.py:13
  71.2 6.1 %collective-permute-start.9 = (bf16[128,256]{1,0:T(8,128)(2,1)S(1)}, bf16[128,256]{1,0:T(8,128)(2,1)S(1)}, u32[]{:S(2)}, u32[]{:S(2)}) collective-permute-start(bf16[128,256]{1,0:T(8,128)(2,1)S(1)} %fusion.30), channel_id=1, source_target_pairs={{4,0},{8,4},{12,8},{0,12},{5,1},{9,5},{13,9},{1,13},{6,2},{10,6},{... | collective-permute-start | bytes 196616 | tf_op jit(solution)/shard_map/ppermute | solution.py:13
  75.4 6.1 %collective-permute-start.8 = (bf16[128,256]{1,0:T(8,128)(2,1)S(1)}, bf16[128,256]{1,0:T(8,128)(2,1)S(1)}, u32[]{:S(2)}, u32[]{:S(2)}) collective-permute-start(bf16[128,256]{1,0:T(8,128)(2,1)S(1)} %fusion.30), channel_id=1, source_target_pairs={{12,0},{0,4},{4,8},{8,12},{13,1},{1,5},{5,9},{9,13},{14,2},{2,6},{... | collective-permute-start | bytes 196616 | tf_op jit(solution)/shard_map/ppermute | solution.py:13
  82.1 0.7 copy-start.16
  82.9 3.9 %copy-start.3 = (f32[512,256]{1,0:T(8,128)S(1)}, f32[512,256]{1,0:T(8,128)}, u32[]{:S(2)}) copy-start(f32[512,256]{1,0:T(8,128)} %copy-done.2) | copy-start | bytes 1572868
  86.7 1.0 copy-start.5
Sparse Core Ops, SparseCore 0:
  88.9 58.4 reduce-scatter.3
where the time goes:
time: 199 us
  waiting for transfers between devices  68.4 us (34%)
  blocking collectives  50.3 us (25%)
  starting transfers between devices  20.7 us (10%)
  matrix products  20.2 us (10%)
  between operations  14.5 us (7%)
  local copies, waits for them, and re-layouts  12.9 us (6%)
  other arithmetic  11.6 us (6%)
    unnamed x2, waiting for transfers between devices  46.8 us
    all_gather x1, blocking collectives, per_device(): lax.all_gather(weight_part, ('regroup', 'loop'), axis=0, tiled=True)  31.3 us
    ppermute x10, waiting for transfers between devices, shifted(): return lax.ppermute(block, axis, route)  18 us
    ppermute x10, starting transfers between devices, shifted(): return lax.ppermute(block, axis, route)  17.2 us
    psum x1, blocking collectives, per_device(): weight_part = lax.psum(weight_part, 'replica')  11.5 us
    dot_general x2, matrix products, from_nets(): jnp.einsum('tr,tif->rif', row_hot, per_tile, precision=high)  7.83 us
    dot_general x2, matrix products, to_nets(): return jnp.einsum('tc,tjf->cjf', hot, per_tile, precision=high)  7.66 us
    all_to_all x1, blocking collectives, per_device(): lax.all_to_all(grad_rows[None, None], 'regroup', split_axis=3, concat_axi...  7.56 us
  transfers between devices with their start and end apart: 12, of which 9 were waited for; matrix products, arithmetic and copies ran while one was open for 9% of the time, Pallas kernels for 0%

commit v1 on v0

--- a/solution.py
+++ b/solution.py
@@ -18,7 +18,12 @@
 
 
 def per_device(features, weight, tiles, tile_row, tile_col, tile_width, cotangent):
-    cell_rows = lax.all_to_all(features, "regroup", split_axis=2, concat_axis=3, tiled=True)[0, 0]
+    cell_rows = jnp.concatenate(
+        lax.all_to_all(
+            jnp.stack(jnp.split(features, lax.axis_size("regroup"), axis=2)), "regroup", 0, 0
+        ),
+        axis=3,
+    )[0, 0]
     cells, width = cell_rows.shape
     edge = tiles.shape[-1]
     blocks = cells // edge

time: 199 us -> 187 us (0.940)
  other arithmetic: 11.6 us -> 7.46 us
  local copies, waits for them, and re-layouts: 12.9 us -> 9.39 us
  waiting for transfers between devices: 68.4 us -> 66.1 us
  starting transfers between devices: 20.7 us -> 18.7 us
    reduce_scatter x0 -> x1, waiting for transfers between devices: none -> 46.9 us  [per_device(): lax.psum_scatter(weight_term, ('regroup', 'loop'), scatter_dimension=0, t...]
    unnamed x2 -> x1, waiting for transfers between devices: 46.8 us -> 0.02 us
    unnamed x51 -> x49, local copies, waits for them, and re-layouts: 7.11 us -> 2.71 us
    all_to_all x1, waiting for transfers between devices: 3.61 us -> 0.01 us  [per_device(): lax.all_to_all(jnp.stack(jnp.split(features, lax.axis_size('regroup'), ax...]
    ppermute x10, starting transfers between devices: 17.2 us -> 14.5 us  [shifted(): return lax.ppermute(block, axis, route)]
    unnamed x2 -> x1, other arithmetic: 4.45 us -> 2.21 us
  transfers between devices with their start and end apart: 12 -> 12, of which waited for: 9 -> 9; matrix products, arithmetic and copies ran while one was open for 9% -> 8% of each run, Pallas kernels for 0% -> 0%
where the time goes in v1:
time: 187 us
  waiting for transfers between devices  66.1 us (35%)
  blocking collectives  49.5 us (26%)
  matrix products  20.9 us (11%)
  starting transfers between devices  18.7 us (10%)
  between operations  14.5 us (8%)
  local copies, waits for them, and re-layouts  9.39 us (5%)
  other arithmetic  7.46 us (4%)
    reduce_scatter x1, waiting for transfers between devices, per_device(): lax.psum_scatter(weight_term, ('regroup', 'loop'), scatter_dimension=0, t...  46.9 us
    all_gather x1, blocking collectives, per_device(): lax.all_gather(weight_part, ('regroup', 'loop'), axis=0, tiled=True)  31.1 us
    ppermute x10, waiting for transfers between devices, shifted(): return lax.ppermute(block, axis, route)  19.2 us
    ppermute x10, starting transfers between devices, shifted(): return lax.ppermute(block, axis, route)  14.5 us
    psum x1, blocking collectives, per_device(): weight_part = lax.psum(weight_part, 'replica')  10.8 us
    dot_general x2, matrix products, from_nets(): jnp.einsum('tr,tif->rif', row_hot, per_tile, precision=high)  7.81 us
    dot_general x2, matrix products, to_nets(): return jnp.einsum('tc,tjf->cjf', hot, per_tile, precision=high)  7.66 us
    all_to_all x1, blocking collectives, per_device(): lax.all_to_all(grad_rows[None, None], 'regroup', split_axis=3, concat_axi...  7.56 us
  transfers between devices with their start and end apart: 12, of which 9 were waited for; matrix products, arithmetic and copies ran while one was open for 8% of the time, Pallas kernels for 0%

profile of v1, /device:TPU:0, one launch (start us, length us, event | category | flops | bytes accessed | tf_op | source)
XLA Modules:
  0.0 186.5 jit_solution(3267168057996213915)
XLA Ops:
  7.2 1.1 fusion.55
  8.5 0.7 pad_maximum_fusion
  9.3 4.2 %all-to-all-start = ((bf16[2,1,1,512,128]{3,4,2,1,0:T(8,128)(2,1)}), bf16[2,1,1,512,128]{3,4,2,1,0:T(8,128)(2,1)S(1)}, u32[]{:S(2)}, u32[]{:S(2)}) async-start(bf16[2,1,1,512,128]{3,4,2,1,0:T(8,128)(2,1)} %pad_maximum_fusion), calls=%async_computation | async-start | bytes 524288 | tf_op jit(solution)/shard_map/all_to_all | solution.py:22
  14.8 4.3 %collective-permute-start.3 = (bf16[128]{0:T(256)(128)(2,1)}, bf16[128]{0:T(256)(128)(2,1)}, u32[]{:S(2)}, u32[]{:S(2)}) collective-permute-start(bf16[128]{0:T(256)(128)(2,1)} %get-tuple-element.16), channel_id=1, source_target_pairs={{4,0},{8,4},{12,8},{0,12},{5,1},{9,5},{13,9},{1,13},{6,2},{10,6},{... | collective-permute-start | bytes 776 | tf_op jit(solution)/shard_map/ppermute | solution.py:13
  19.8 0.7 copy.91
  20.6 1.1 divide_convert_fusion
  22.4 0.8 fusion.23
  23.1 3.8 %fusion.9 = bf16[3,128,256]{2,0,1:T(4,128)(2,1)S(1)} fusion(f32[32,128,256]{2,1,0:T(8,128)S(1)} %fusion.23, s32[32]{0:T(128)S(1)} %copy-done.10), kind=kOutput, calls=%fused_computation.17 | convolution fusion | flops 37847136 | bytes 4391040 | tf_op jit(solution)/shard_map/tc,tjf->cjf/dot_general | solution.py:52
  27.3 3.9 %collective-permute-start.1 = (bf16[128,256]{1,0:T(8,128)(2,1)S(1)}, bf16[128,256]{1,0:T(8,128)(2,1)S(1)}, u32[]{:S(2)}, u32[]{:S(2)}) collective-permute-start(bf16[128,256]{1,0:T(8,128)(2,1)S(1)} %bitcast.140), channel_id=1, source_target_pairs={{4,0},{8,4},{12,8},{0,12},{5,1},{9,5},{13,9},{1,13},{6,2},{10,6},{... | collective-permute-start | bytes 196616 | tf_op jit(solution)/shard_map/ppermute | solution.py:13
  31.9 1.1 collective-permute-done.1
  33.0 4.8 %collective-permute-done = bf16[128,256]{1,0:T(8,128)(2,1)S(1)} collective-permute-done((bf16[128,256]{1,0:T(8,128)(2,1)S(1)}, bf16[128,256]{1,0:T(8,128)(2,1)S(1)}, u32[]{:S(2)}, u32[]{:S(2)}) %collective-permute-start) | collective-permute-done | bytes 65568 | tf_op jit(solution)/shard_map/ppermute | solution.py:13
  38.0 2.0 %collective-permute-start.4 = (bf16[128,256]{1,0:T(8,128)(2,1)S(1)}, bf16[128,256]{1,0:T(8,128)(2,1)S(1)}, u32[]{:S(2)}, u32[]{:S(2)}) collective-permute-start(bf16[128,256]{1,0:T(8,128)(2,1)S(1)} %fusion.27), channel_id=1, source_target_pairs={{12,0},{0,4},{4,8},{8,12},{13,1},{1,5},{5,9},{9,13},{14,2},{2,6},{... | collective-permute-start | bytes 196616 | tf_op jit(solution)/shard_map/ppermute | solution.py:13
  40.0 2.2 %collective-permute-done.5 = bf16[128,256]{1,0:T(8,128)(2,1)S(1)} collective-permute-done((bf16[128,256]{1,0:T(8,128)(2,1)S(1)}, bf16[128,256]{1,0:T(8,128)(2,1)S(1)}, u32[]{:S(2)}, u32[]{:S(2)}) %collective-permute-start.5) | collective-permute-done | bytes 65568 | tf_op jit(solution)/shard_map/ppermute | solution.py:13
  42.3 2.0 %collective-permute-done.4 = bf16[128,256]{1,0:T(8,128)(2,1)S(1)} collective-permute-done((bf16[128,256]{1,0:T(8,128)(2,1)S(1)}, bf16[128,256]{1,0:T(8,128)(2,1)S(1)}, u32[]{:S(2)}, u32[]{:S(2)}) %collective-permute-start.4) | collective-permute-done | bytes 65568 | tf_op jit(solution)/shard_map/ppermute | solution.py:13
  45.9 4.0 %fusion.19 = (f32[4,128]{0,1:T(8,128)S(1)}, f32[4,128,256]{2,0,1:T(4,128)S(1)}) fusion(f32[4,128]{0,1:T(8,128)S(1)} %copy-done.8, f32[32,128,256]{2,1,0:T(8,128)S(1)} %fusion.22, s32[32]{0:T(128)S(1)} %bitcast.151), kind=kOutput, calls=%fused_computation.38 | convolution fusion | flops 50724480 | bytes 4722816 | tf_op jit(solution)/shard_map/tr,tif->rif/dot_general | solution.py:59
  50.1 1.1 multiply_reduce_fusion
  52.7 0.8 fusion.21
  53.5 3.8 %fusion.2 = bf16[3,128,256]{2,0,1:T(4,128)(2,1)S(1)} fusion(f32[32,128,256]{2,1,0:T(8,128)S(1)} %fusion.21, s32[32]{0:T(128)S(1)} %copy-done.11), kind=kOutput, calls=%fused_computation.6 | convolution fusion | flops 37748832 | bytes 4391040 | tf_op jit(solution)/shard_map/tc,tjf->cjf/dot_general | solution.py:52
  57.5 2.0 %collective-permute-start.6 = (bf16[128,256]{1,0:T(8,128)(2,1)S(1)}, bf16[128,256]{1,0:T(8,128)(2,1)S(1)}, u32[]{:S(2)}, u32[]{:S(2)}) collective-permute-start(bf16[128,256]{1,0:T(8,128)(2,1)S(1)} %get-tuple-element.13), channel_id=1, source_target_pairs={{12,0},{0,4},{4,8},{8,12},{13,1},{1,5},{5,9},{9,13},{14,2},{2,6},{... | collective-permute-start | bytes 196616 | tf_op jit(solution)/shard_map/ppermute | solution.py:13
  59.5 2.6 %collective-permute-done.7 = bf16[128,256]{1,0:T(8,128)(2,1)S(1)} collective-permute-done((bf16[128,256]{1,0:T(8,128)(2,1)S(1)}, bf16[128,256]{1,0:T(8,128)(2,1)S(1)}, u32[]{:S(2)}, u32[]{:S(2)}) %collective-permute-start.7) | collective-permute-done | bytes 65568 | tf_op jit(solution)/shard_map/ppermute | solution.py:13
  62.1 1.7 collective-permute-done.6
  64.5 1.4 collective-permute-start.8
  66.0 2.2 %collective-permute-done.9 = bf16[128,256]{1,0:T(8,128)(2,1)S(1)} collective-permute-done((bf16[128,256]{1,0:T(8,128)(2,1)S(1)}, bf16[128,256]{1,0:T(8,128)(2,1)S(1)}, u32[]{:S(2)}, u32[]{:S(2)}) %collective-permute-start.9) | collective-permute-done | bytes 65568 | tf_op jit(solution)/shard_map/ppermute | solution.py:13
  68.2 2.4 %collective-permute-done.8 = bf16[128,256]{1,0:T(8,128)(2,1)S(1)} collective-permute-done((bf16[128,256]{1,0:T(8,128)(2,1)S(1)}, bf16[128,256]{1,0:T(8,128)(2,1)S(1)}, u32[]{:S(2)}, u32[]{:S(2)}) %collective-permute-start.8) | collective-permute-done | bytes 65568 | tf_op jit(solution)/shard_map/ppermute | solution.py:13
  72.1 3.8 %fusion = f32[4,128,256]{2,0,1:T(4,128)S(1)} fusion(f32[32,128,256]{2,1,0:T(8,128)S(1)} %fusion.20, s32[32]{0:T(128)S(1)} %bitcast.152), kind=kOutput, calls=%fused_computation.4 | convolution fusion | flops 50331776 | bytes 4718720 | tf_op jit(solution)/shard_map/tr,tif->rif/dot_general | solution.py:59
  76.8 0.9 fusion.56
  79.0 2.2 %reduce.1 = bf16[256,512]{1,0:T(8,128)(2,1)S(1)} reduce(bf16[256,1,1,512]{3,2,1,0:T(2,128)(2,1)S(1)} %bitcast.131, bf16[]{:T(256)} %broadcast.232), dimensions={1,2}, to_apply=%bitcast.108.reduce_sub_computation | reduce | bytes 524290
  81.4 7.6 %all_to_all.23 = bf16[2,2,32768]{2,1,0:T(2,128)(2,1)S(1)} all-to-all(bf16[2,2,32768]{2,1,0:T(2,128)(2,1)S(1)} %reshape.233), channel_id=1, replica_groups=mesh['regroup'=2,'loop'=4,'replica'=4] {'regroup'}, dimensions={0} | all-to-all | bytes 524288 | tf_op jit(solution)/shard_map/all_to_all | solution.py:113
  89.3 0.8 copy.99
  90.2 46.9 %reduce-scatter.2.cloned.1.call-done = f32[32,256]{1,0:T(8,128)} async-done(((f32[256,256]{1,0:T(8,128)}), f32[32,256]{1,0:T(8,128)}) %reduce-scatter.2.cloned.1.call-update) | async-done | bytes 32784 | tf_op jit(solution)/shard_map/reduce_scatter | solution.py:117
  137.0 10.8 %psum.7 = f32[32,256]{1,0:T(8,128)S(1)} all-reduce(f32[32,256]{1,0:T(8,128)} %reduce-scatter.2.cloned.1.call-done), channel_id=1, replica_groups=mesh['regroup'=2,'loop'=4,'replica'=4] {'replica'}, use_global_device_ids=true, to_apply=%region_5.6 | all-reduce | flops 8192 | bytes 65536 | tf_op jit(solution)/shard_map/psum | solution.py:120
  147.8 31.1 %all_gather.3 = f32[256,256]{1,0:T(8,128)S(1)} all-gather(f32[32,256]{1,0:T(8,128)S(1)} %psum.7), channel_id=1, replica_groups=mesh['regroup'=2,'loop'=4,'replica'=4] {'regroup','loop'}, dimensions={0}, use_global_device_ids=true | all-gather | bytes 294912 | tf_op jit(solution)/shard_map/all_gather | solution.py:121
  (93 shorter events, 12.9 us)
Async XLA Ops:
  7.2 13.4 %copy-start = (bf16[256,256]{1,0:T(8,128)(2,1)S(1)}, bf16[256,256]{1,0:T(8,128)(2,1)}, u32[]{:S(2)}) copy-start(bf16[256,256]{1,0:T(8,128)(2,1)} %param.8) | copy-start | bytes 393220
  7.2 6.3 %copy-start.17 = (s32[1,1,1,32]{3,2,1,0:T(1,128)S(1)}, s32[1,1,1,32]{3,2,1,0:T(1,128)}, u32[]{:S(2)}) copy-start(s32[1,1,1,32]{3,2,1,0:T(1,128)} %param.12) | copy-start | bytes 388
  7.2 6.4 %copy-start.1 = (bf16[1,1,1,32,128,128]{5,4,3,2,1,0:T(8,128)(2,1)S(1)}, bf16[1,1,1,32,128,128]{5,4,3,2,1,0:T(8,128)(2,1)}, u32[]{:S(2)}) copy-start(bf16[1,1,1,32,128,128]{5,4,3,2,1,0:T(8,128)(2,1)} %param.9) | copy-start | bytes 3145732
  7.2 6.8 %copy-start.19 = (s32[1,1,1,32]{3,2,1,0:T(1,128)S(1)}, s32[1,1,1,32]{3,2,1,0:T(1,128)}, u32[]{:S(2)}) copy-start(s32[1,1,1,32]{3,2,1,0:T(1,128)} %param.11) | copy-start | bytes 388
  7.2 11.9 %copy-start.14 = (s32[1,1,1,32]{3,2,1,0:T(1,128)S(1)}, s32[1,1,1,32]{3,2,1,0:T(1,128)}, u32[]{:S(2)}) copy-start(s32[1,1,1,32]{3,2,1,0:T(1,128)} %param.10) | copy-start | bytes 388
  9.3 11.3 %all-to-all-start = ((bf16[2,1,1,512,128]{3,4,2,1,0:T(8,128)(2,1)}), bf16[2,1,1,512,128]{3,4,2,1,0:T(8,128)(2,1)S(1)}, u32[]{:S(2)}, u32[]{:S(2)}) async-start(bf16[2,1,1,512,128]{3,4,2,1,0:T(8,128)(2,1)} %pad_maximum_fusion), calls=%async_computation | async-start | bytes 524288 | tf_op jit(solution)/shard_map/all_to_all | solution.py:22
  13.5 123.5 %reduce-scatter.2.cloned.1.call-start = ((), (), s32[]{:S(2)}) async-start(), calls=%async_computation.3 | async-start | bytes 294912 | tf_op jit(solution)/shard_map/reduce_scatter | solution.py:117
  14.0 5.1 %copy-start.9 = (s32[32]{0:T(128)}, s32[32]{0:T(128)S(1)}, u32[]{:S(2)}) copy-start(s32[32]{0:T(128)S(1)} %compare_select_fusion.8) | copy-start | bytes 388
  14.8 16.5 %collective-permute-start.3 = (bf16[128]{0:T(256)(128)(2,1)}, bf16[128]{0:T(256)(128)(2,1)}, u32[]{:S(2)}, u32[]{:S(2)}) collective-permute-start(bf16[128]{0:T(256)(128)(2,1)} %get-tuple-element.16), channel_id=1, source_target_pairs={{4,0},{8,4},{12,8},{0,12},{5,1},{9,5},{13,9},{1,13},{6,2},{10,6},{... | collective-permute-start | bytes 776 | tf_op jit(solution)/shard_map/ppermute | solution.py:13
  19.1 12.2 %collective-permute-start.2 = (bf16[128]{0:T(256)(128)(2,1)}, bf16[128]{0:T(256)(128)(2,1)}, u32[]{:S(2)}, u32[]{:S(2)}) collective-permute-start(bf16[128]{0:T(256)(128)(2,1)} %get-tuple-element.15), channel_id=1, source_target_pairs={{12,0},{0,4},{4,8},{8,12},{13,1},{1,5},{5,9},{9,13},{14,2},{2,6},{... | collective-permute-start | bytes 776 | tf_op jit(solution)/shard_map/ppermute | solution.py:13
  20.5 1.1 copy-start.4
  22.3 0.8 copy-start.10
  23.1 16.9 %copy-start.18 = (s32[32]{0:T(128)S(1)}, s32[32]{0:T(128)}, u32[]{:S(2)}) copy-start(s32[32]{0:T(128)} %fusion.43) | copy-start | bytes 388
  27.3 5.8 %collective-permute-start.1 = (bf16[128,256]{1,0:T(8,128)(2,1)S(1)}, bf16[128,256]{1,0:T(8,128)(2,1)S(1)}, u32[]{:S(2)}, u32[]{:S(2)}) collective-permute-start(bf16[128,256]{1,0:T(8,128)(2,1)S(1)} %bitcast.140), channel_id=1, source_target_pairs={{4,0},{8,4},{12,8},{0,12},{5,1},{9,5},{13,9},{1,13},{6,2},{10,6},{... | collective-permute-start | bytes 196616 | tf_op jit(solution)/shard_map/ppermute | solution.py:13
  31.2 6.7 %collective-permute-start = (bf16[128,256]{1,0:T(8,128)(2,1)S(1)}, bf16[128,256]{1,0:T(8,128)(2,1)S(1)}, u32[]{:S(2)}, u32[]{:S(2)}) collective-permute-start(bf16[128,256]{1,0:T(8,128)(2,1)S(1)} %bitcast.141), channel_id=1, source_target_pairs={{12,0},{0,4},{4,8},{8,12},{13,1},{1,5},{5,9},{9,13},{14,2},{2,6},{... | collective-permute-start | bytes 196616 | tf_op jit(solution)/shard_map/ppermute | solution.py:13
  31.9 12.4 %copy-start.12 = (f32[128]{0:T(128)}, f32[128]{0:T(128)S(1)}, u32[]{:S(2)}) copy-start(f32[128]{0:T(128)S(1)} %fusion.48) | copy-start | bytes 1540
  38.0 4.3 %collective-permute-start.5 = (bf16[128,256]{1,0:T(8,128)(2,1)S(1)}, bf16[128,256]{1,0:T(8,128)(2,1)S(1)}, u32[]{:S(2)}, u32[]{:S(2)}) collective-permute-start(bf16[128,256]{1,0:T(8,128)(2,1)S(1)} %fusion.27), channel_id=1, source_target_pairs={{4,0},{8,4},{12,8},{0,12},{5,1},{9,5},{13,9},{1,13},{6,2},{10,6},{... | collective-permute-start | bytes 196616 | tf_op jit(solution)/shard_map/ppermute | solution.py:13
  38.0 6.3 %collective-permute-start.4 = (bf16[128,256]{1,0:T(8,128)(2,1)S(1)}, bf16[128,256]{1,0:T(8,128)(2,1)S(1)}, u32[]{:S(2)}, u32[]{:S(2)}) collective-permute-start(bf16[128,256]{1,0:T(8,128)(2,1)S(1)} %fusion.27), channel_id=1, source_target_pairs={{12,0},{0,4},{4,8},{8,12},{13,1},{1,5},{5,9},{9,13},{14,2},{2,6},{... | collective-permute-start | bytes 196616 | tf_op jit(solution)/shard_map/ppermute | solution.py:13
  45.0 0.8 copy-start.8
  45.0 0.8 copy-start.15
  45.9 4.2 %copy-start.6 = (f32[512,256]{1,0:T(8,128)S(1)}, f32[512,256]{1,0:T(8,128)}, u32[]{:S(2)}) copy-start(f32[512,256]{1,0:T(8,128)} %get-tuple-element.18) | copy-start | bytes 1572868
  45.9 4.2 %copy-start.7 = (bf16[1,1,1,512,256]{4,3,2,1,0:T(8,128)(2,1)S(1)}, bf16[1,1,1,512,256]{4,3,2,1,0:T(8,128)(2,1)}, u32[]{:S(2)}) copy-start(bf16[1,1,1,512,256]{4,3,2,1,0:T(8,128)(2,1)} %param.13) | copy-start | bytes 786436
  51.2 0.8 copy-start.2
  52.7 0.8 copy-start.11
  53.5 10.3 %copy-start.13 = (f32[128]{0:T(128)S(1)}, f32[128]{0:T(128)}, u32[]{:S(2)}) copy-start(f32[128]{0:T(128)} %copy-done.12) | copy-start | bytes 1540
  57.4 4.7 %collective-permute-start.7 = (bf16[128,256]{1,0:T(8,128)(2,1)S(1)}, bf16[128,256]{1,0:T(8,128)(2,1)S(1)}, u32[]{:S(2)}, u32[]{:S(2)}) collective-permute-start(bf16[128,256]{1,0:T(8,128)(2,1)S(1)} %get-tuple-element.14), channel_id=1, source_target_pairs={{4,0},{8,4},{12,8},{0,12},{5,1},{9,5},{13,9},{1,13},{6,2},{10,6},{... | collective-permute-start | bytes 196616 | tf_op jit(solution)/shard_map/ppermute | solution.py:13
  57.5 6.3 %collective-permute-start.6 = (bf16[128,256]{1,0:T(8,128)(2,1)S(1)}, bf16[128,256]{1,0:T(8,128)(2,1)S(1)}, u32[]{:S(2)}, u32[]{:S(2)}) collective-permute-start(bf16[128,256]{1,0:T(8,128)(2,1)S(1)} %get-tuple-element.13), channel_id=1, source_target_pairs={{12,0},{0,4},{4,8},{8,12},{13,1},{1,5},{5,9},{9,13},{14,2},{2,6},{... | collective-permute-start | bytes 196616 | tf_op jit(solution)/shard_map/ppermute | solution.py:13
  63.9 4.3 %collective-permute-start.9 = (bf16[128,256]{1,0:T(8,128)(2,1)S(1)}, bf16[128,256]{1,0:T(8,128)(2,1)S(1)}, u32[]{:S(2)}, u32[]{:S(2)}) collective-permute-start(bf16[128,256]{1,0:T(8,128)(2,1)S(1)} %fusion.30), channel_id=1, source_target_pairs={{4,0},{8,4},{12,8},{0,12},{5,1},{9,5},{13,9},{1,13},{6,2},{10,6},{... | collective-permute-start | bytes 196616 | tf_op jit(solution)/shard_map/ppermute | solution.py:13
  64.5 6.1 %collective-permute-start.8 = (bf16[128,256]{1,0:T(8,128)(2,1)S(1)}, bf16[128,256]{1,0:T(8,128)(2,1)S(1)}, u32[]{:S(2)}, u32[]{:S(2)}) collective-permute-start(bf16[128,256]{1,0:T(8,128)(2,1)S(1)} %fusion.30), channel_id=1, source_target_pairs={{12,0},{0,4},{4,8},{8,12},{13,1},{1,5},{5,9},{9,13},{14,2},{2,6},{... | collective-permute-start | bytes 196616 | tf_op jit(solution)/shard_map/ppermute | solution.py:13
  71.3 0.7 copy-start.16
  72.0 3.9 %copy-start.3 = (f32[512,256]{1,0:T(8,128)S(1)}, f32[512,256]{1,0:T(8,128)}, u32[]{:S(2)}) copy-start(f32[512,256]{1,0:T(8,128)} %copy-done.2) | copy-start | bytes 1572868
  75.9 1.0 copy-start.5
Sparse Core Ops, SparseCore 0:
  77.9 59.0 reduce-scatter.1
